TPU v7x, 32 devices: a whole 2x2x4 slice. The times are simulated.
32 devices in a mesh: replica: 8 (over z, x), group: 4 (over y, core).
Axes of the slice: x: 2, y: 2, z: 4, core: 2. Of those that a mesh axis runs over, the one named last changes fastest.
Arguments:
- inputs: bfloat16 [8192, 576], P(('replica', 'group')), may hold values from -6 to 6
- segment_ids: int32 [32, 256], P(('replica', 'group')), may hold values from 0 to 2, never falling along the last dimension, each value on 1 to 128 neighbouring positions
- live_counts: int32 [32], P(('replica', 'group')), may hold values from 128 to 256, as said below
- cotangent: bfloat16 [8192, 576], P(('replica', 'group')), may hold values from -6 to 6
- w_query: bfloat16 [576, 576], P('group'), may hold values from -0.25 to 0.25
- w_key: bfloat16 [576, 192], P('group'), may hold values from -0.25 to 0.25
- w_value: bfloat16 [576, 192], P('group'), may hold values from -0.25 to 0.25
- w_out: bfloat16 [576, 576], P(None, 'group'), may hold values from -0.75 to 0.75
- w_gate: bfloat16 [576, 1536], P('group'), may hold values from -0.25 to 0.25
- w_up: bfloat16 [576, 1536], P('group'), may hold values from -0.25 to 0.25
- w_down: bfloat16 [1536, 576], P(None, 'group'), may hold values from -0.15625 to 0.15625
- norm_attn: bfloat16 [576], P('group'), may hold values from 0.5 to 1.5
- norm_ffn: bfloat16 [576], P('group'), may hold values from 0.5 to 1.5
Outputs:
- output: bfloat16 [8192, 576], P(('replica', 'group'))
- grad_input: float32 [8192, 576], P(('replica', 'group'))
- grad_query: float32 [576, 576], P('group')
- grad_key: float32 [576, 192], P('group')
- grad_value: float32 [576, 192], P('group')
- grad_out: float32 [576, 576], P(None, 'group')
- grad_gate: float32 [576, 1536], P('group')
- grad_up: float32 [576, 1536], P('group')
- grad_down: float32 [1536, 576], P(None, 'group')
- grad_norm_attn: float32 [576], P('group')
- grad_norm_ffn: float32 [576], P('group')
Inputs may be any that keep to these rules, and one draw needn't show every extreme that they name: `segment_ids`: within each row the ids never fall; every id appears; each sequence has 1 to 128 slots and one has exactly 128. `live_counts`: some device is full and some holds exactly 128 real tokens.
All inputs are finite; a program needn't handle non-finite values.
Results may differ from a plain program's by a relative error of at most 0.012.
Values may be sent and summed in bfloat16 or wider, within the bound.
A program may use at most 128 MiB of HBM per device.

v0:
```python
import math

import jax
import jax.numpy as jnp
from jax import lax
from jax.sharding import PartitionSpec as P

HEADS = 9
KV_HEADS = 3
HEAD = 64


norm_eps = 1e-05
rope_base = 100000.0
masked_value = -1e30


def contract(pattern, left_op, right_op):
    return jnp.einsum(pattern, left_op, right_op, preferred_element_type=jnp.float32)


def matmul(left_op, right_op):
    return jnp.dot(left_op, right_op, preferred_element_type=jnp.float32)


def rope_tables(segment_row):
    row_count = segment_row.shape[0]
    seg_first = jnp.searchsorted(segment_row, segment_row, side="left")
    offsets = (jnp.arange(row_count, dtype=jnp.int32) - seg_first).astype(jnp.float32)
    frequency = jnp.exp(
        jnp.arange(HEAD // 2, dtype=jnp.float32) * (-2.0 * math.log(rope_base) / HEAD)
    )
    angles = offsets[:, None] * frequency[None, :]
    return (jnp.cos(angles)[:, None, :], jnp.sin(angles)[:, None, :])


def rotate(values, cosine, sine):
    half_size = values.shape[-1] // 2
    first_half = values[..., :half_size]
    second_half = values[..., half_size:]
    return jnp.concatenate(
        [first_half * cosine - second_half * sine, second_half * cosine + first_half * sine],
        axis=-1,
    )


def unrotate(values, cosine, sine):
    half_size = values.shape[-1] // 2
    first_half = values[..., :half_size]
    second_half = values[..., half_size:]
    return jnp.concatenate(
        [first_half * cosine + second_half * sine, second_half * cosine - first_half * sine],
        axis=-1,
    )


def norm_forward(values):
    inverse = lax.rsqrt(jnp.mean(values * values, axis=-1, keepdims=True) + norm_eps)
    return (values * inverse, inverse)


def norm_backward(grad_out, normed, gain, inverse):
    grad_normed = grad_out * gain
    grad_in = inverse * (
        grad_normed - normed * jnp.mean(grad_normed * normed, axis=-1, keepdims=True)
    )
    return (grad_in, jnp.sum(grad_out * normed, axis=0))


def block_mask(segment_row, live_count, row_start, row_stop):
    position = jnp.arange(row_stop, dtype=jnp.int32)
    same_seq = segment_row[row_start:row_stop, None] == segment_row[None, :row_stop]
    causal = position[None, :] <= position[row_start:row_stop, None]
    key_ok = (position[None, :] < live_count) | (
        position[None, :] == position[row_start:row_stop, None]
    )
    return same_seq & causal & key_ok


def attend(queries, keys_rot, values, segment_row, live_count):
    row_count = queries.shape[0]
    blk_size = min(512, row_count)
    score_scale = queries.shape[-1] ** (-0.5)
    allowed = block_mask(segment_row, live_count, 0, blk_size)
    head_outs = []
    head_totals = []
    for kv_group in range(keys_rot.shape[1]):
        scores = (
            contract("qhd,kd->hqk", queries[0:blk_size, kv_group], keys_rot[:blk_size, kv_group])
            * score_scale
        )
        scores = jnp.where(allowed[None], scores, masked_value)
        row_max = jnp.max(scores, axis=2, keepdims=True)
        log_total = row_max + jnp.log(jnp.sum(jnp.exp(scores - row_max), axis=2, keepdims=True))
        probs = jnp.exp(scores - log_total).astype(jnp.bfloat16)
        head_outs.append(
            contract("hqk,kd->qhd", probs, values[:blk_size, kv_group]).astype(jnp.bfloat16)
        )
        head_totals.append(log_total[:, :, 0])
    out_blocks = jnp.stack(head_outs, axis=1)
    total_blocks = jnp.stack(head_totals, axis=0)
    return (out_blocks, total_blocks)


def attend_back(
    queries, keys_rot, values, segment_row, live_count, attn_out, log_totals, grad_attn
):
    row_count = queries.shape[0]
    blk_size = min(512, row_count)
    score_scale = queries.shape[-1] ** (-0.5)
    deltas = jnp.sum(grad_attn.astype(jnp.float32) * attn_out.astype(jnp.float32), axis=-1)
    grad_keys = jnp.zeros(keys_rot.shape, jnp.float32)
    grad_values = jnp.zeros(values.shape, jnp.float32)
    allowed = block_mask(segment_row, live_count, 0, blk_size)
    head_grads = []
    for kv_group in range(keys_rot.shape[1]):
        query_blk = queries[0:blk_size, kv_group]
        grad_blk = grad_attn[0:blk_size, kv_group]
        scores = contract("qhd,kd->hqk", query_blk, keys_rot[:blk_size, kv_group]) * score_scale
        scores = jnp.where(allowed[None], scores, masked_value)
        probs = jnp.exp(scores - log_totals[kv_group][:, 0:blk_size, None])
        probs_bf = probs.astype(jnp.bfloat16)
        grad_probs = contract("qhd,kd->hqk", grad_blk, values[:blk_size, kv_group])
        delta_blk = jnp.transpose(deltas[0:blk_size, kv_group])
        grad_scores = (probs * (grad_probs - delta_blk[:, :, None]) * score_scale).astype(
            jnp.bfloat16
        )
        head_grads.append(contract("hqk,kd->qhd", grad_scores, keys_rot[:blk_size, kv_group]))
        grad_keys = grad_keys.at[:blk_size, kv_group].add(
            contract("hqk,qhd->kd", grad_scores, query_blk)
        )
        grad_values = grad_values.at[:blk_size, kv_group].add(
            contract("hqk,qhd->kd", probs_bf, grad_blk)
        )
    query_blocks = jnp.stack(head_grads, axis=1)
    return (query_blocks, grad_keys, grad_values)


def layer_forward(inputs, segment_row, live_count, weights):
    w_query, w_key, w_value, w_out, w_gate, w_up, w_down, norm_attn, norm_ffn = weights
    row_count = inputs.shape[0]
    group_size = HEADS // KV_HEADS
    live_rows = jnp.arange(row_count, dtype=jnp.int32) < live_count
    input_f = inputs.astype(jnp.float32)
    normed_one, inverse_one = norm_forward(input_f)
    hidden_one = (normed_one * norm_attn.astype(jnp.float32)).astype(jnp.bfloat16)
    cosine, sine = rope_tables(segment_row)
    query_raw = matmul(hidden_one, w_query).reshape(row_count, HEADS, HEAD)
    key_raw = matmul(hidden_one, w_key).reshape(row_count, KV_HEADS, HEAD)
    value_bf = matmul(hidden_one, w_value).astype(jnp.bfloat16).reshape(row_count, KV_HEADS, HEAD)
    query_rot = (
        rotate(query_raw, cosine, sine)
        .astype(jnp.bfloat16)
        .reshape(row_count, KV_HEADS, group_size, HEAD)
    )
    key_rot = rotate(key_raw, cosine, sine).astype(jnp.bfloat16)
    attn_out, log_totals = attend(query_rot, key_rot, value_bf, segment_row, live_count)
    attn_flat = attn_out.reshape(row_count, HEADS * HEAD)
    mid_f = input_f + matmul(attn_flat, w_out)
    normed_two, inverse_two = norm_forward(mid_f)
    hidden_two = (normed_two * norm_ffn.astype(jnp.float32)).astype(jnp.bfloat16)
    gate_pre = matmul(hidden_two, w_gate)
    up_pre = matmul(hidden_two, w_up)
    sigmoid_gate = jax.nn.sigmoid(gate_pre)
    silu_gate = gate_pre * sigmoid_gate
    mixed = (silu_gate * up_pre).astype(jnp.bfloat16)
    output = jnp.where(live_rows[:, None], mid_f + matmul(mixed, w_down), 0.0).astype(jnp.bfloat16)
    saved = (
        segment_row,
        live_count,
        live_rows,
        normed_one,
        inverse_one,
        hidden_one,
        cosine,
        sine,
        query_rot,
        key_rot,
        value_bf,
        attn_out,
        log_totals,
        attn_flat,
        normed_two,
        inverse_two,
        hidden_two,
        gate_pre,
        up_pre,
        sigmoid_gate,
        silu_gate,
        mixed,
    )
    return (output, saved)


def layer_backward(saved, cotangent, weights, grad_scale):
    w_query, w_key, w_value, w_out, w_gate, w_up, w_down, norm_attn, norm_ffn = weights
    (
        segment_row,
        live_count,
        live_rows,
        normed_one,
        inverse_one,
        hidden_one,
        cosine,
        sine,
        query_rot,
        key_rot,
        value_bf,
        attn_out,
        log_totals,
        attn_flat,
        normed_two,
        inverse_two,
        hidden_two,
        gate_pre,
        up_pre,
        sigmoid_gate,
        silu_gate,
        mixed,
    ) = saved
    row_count = cotangent.shape[0]
    group_size = HEADS // KV_HEADS
    cot = jnp.where(live_rows[:, None], cotangent, jnp.zeros_like(cotangent))
    grad_down = matmul(mixed.T, cot) * grad_scale
    grad_mixed = matmul(cot, w_down.T)
    grad_gate_pre = (
        grad_mixed * up_pre * (sigmoid_gate * (1.0 + gate_pre * (1.0 - sigmoid_gate)))
    ).astype(jnp.bfloat16)
    grad_up_pre = (grad_mixed * silu_gate).astype(jnp.bfloat16)
    grad_gate = matmul(hidden_two.T, grad_gate_pre) * grad_scale
    grad_up = matmul(hidden_two.T, grad_up_pre) * grad_scale
    grad_hidden_two = matmul(grad_gate_pre, w_gate.T) + matmul(grad_up_pre, w_up.T)
    grad_mid_norm, grad_norm_ffn = norm_backward(
        grad_hidden_two, normed_two, norm_ffn.astype(jnp.float32), inverse_two
    )
    grad_mid = cot.astype(jnp.float32) + grad_mid_norm
    grad_mid_bf = grad_mid.astype(jnp.bfloat16)
    grad_out_w = matmul(attn_flat.T, grad_mid_bf) * grad_scale
    grad_attn = (
        matmul(grad_mid_bf, w_out.T)
        .astype(jnp.bfloat16)
        .reshape(row_count, KV_HEADS, group_size, HEAD)
    )
    grad_query_rot, grad_key_rot, grad_value_f = attend_back(
        query_rot, key_rot, value_bf, segment_row, live_count, attn_out, log_totals, grad_attn
    )
    grad_query_raw = (
        unrotate(grad_query_rot.reshape(row_count, HEADS, HEAD), cosine, sine)
        .astype(jnp.bfloat16)
        .reshape(row_count, HEADS * HEAD)
    )
    grad_key_raw = (
        unrotate(grad_key_rot, cosine, sine)
        .astype(jnp.bfloat16)
        .reshape(row_count, KV_HEADS * HEAD)
    )
    grad_value_bf = grad_value_f.astype(jnp.bfloat16).reshape(row_count, KV_HEADS * HEAD)
    grad_query_w = matmul(hidden_one.T, grad_query_raw) * grad_scale
    grad_key_w = matmul(hidden_one.T, grad_key_raw) * grad_scale
    grad_value_w = matmul(hidden_one.T, grad_value_bf) * grad_scale
    grad_hidden_one = (
        matmul(grad_query_raw, w_query.T)
        + matmul(grad_key_raw, w_key.T)
        + matmul(grad_value_bf, w_value.T)
    )
    grad_in_norm, grad_norm_attn = norm_backward(
        grad_hidden_one, normed_one, norm_attn.astype(jnp.float32), inverse_one
    )
    grad_input = grad_mid + grad_in_norm
    return (
        grad_input,
        (
            grad_query_w,
            grad_key_w,
            grad_value_w,
            grad_out_w,
            grad_gate,
            grad_up,
            grad_down,
            grad_norm_attn * grad_scale,
            grad_norm_ffn * grad_scale,
        ),
    )


def local(
    inputs,
    segment_ids,
    live_counts,
    cotangent,
    w_query,
    w_key,
    w_value,
    w_out,
    w_gate,
    w_up,
    w_down,
    norm_attn,
    norm_ffn,
):
    segment_row = segment_ids[0]
    live_count = live_counts[0]
    token_total = inputs.shape[0] * lax.axis_size("replica") * lax.axis_size("group")
    grad_scale = float(token_total) ** (-0.5)
    weights = (
        lax.all_gather(w_query, "group", axis=0, tiled=True),
        lax.all_gather(w_key, "group", axis=0, tiled=True),
        lax.all_gather(w_value, "group", axis=0, tiled=True),
        lax.all_gather(w_out, "group", axis=1, tiled=True),
        lax.all_gather(w_gate, "group", axis=0, tiled=True),
        lax.all_gather(w_up, "group", axis=0, tiled=True),
        lax.all_gather(w_down, "group", axis=1, tiled=True),
        lax.all_gather(norm_attn, "group", axis=0, tiled=True),
        lax.all_gather(norm_ffn, "group", axis=0, tiled=True),
    )
    output, saved = layer_forward(inputs, segment_row, live_count, weights)
    back_weights = (
        lax.all_gather(w_query, "group", axis=0, tiled=True),
        lax.all_gather(w_key, "group", axis=0, tiled=True),
        lax.all_gather(w_value, "group", axis=0, tiled=True),
        lax.all_gather(w_out, "group", axis=1, tiled=True),
        lax.all_gather(w_gate, "group", axis=0, tiled=True),
        lax.all_gather(w_up, "group", axis=0, tiled=True),
        lax.all_gather(w_down, "group", axis=1, tiled=True),
        lax.all_gather(norm_attn, "group", axis=0, tiled=True),
        lax.all_gather(norm_ffn, "group", axis=0, tiled=True),
    )
    grad_input, block_grads = layer_backward(saved, cotangent, back_weights, grad_scale)
    (
        grad_query_w,
        grad_key_w,
        grad_value_w,
        grad_out_w,
        grad_gate_w,
        grad_up_w,
        grad_down_w,
        grad_gain_one,
        grad_gain_two,
    ) = block_grads
    (
        owned_query,
        owned_key,
        owned_value,
        owned_out,
        owned_gate,
        owned_up,
        owned_down,
        owned_gain_one,
        owned_gain_two,
    ) = (
        lax.psum_scatter(grad_query_w, "group", scatter_dimension=0, tiled=True),
        lax.psum_scatter(grad_key_w, "group", scatter_dimension=0, tiled=True),
        lax.psum_scatter(grad_value_w, "group", scatter_dimension=0, tiled=True),
        lax.psum_scatter(grad_out_w, "group", scatter_dimension=1, tiled=True),
        lax.psum_scatter(grad_gate_w, "group", scatter_dimension=0, tiled=True),
        lax.psum_scatter(grad_up_w, "group", scatter_dimension=0, tiled=True),
        lax.psum_scatter(grad_down_w, "group", scatter_dimension=1, tiled=True),
        lax.psum_scatter(grad_gain_one, "group", scatter_dimension=0, tiled=True),
        lax.psum_scatter(grad_gain_two, "group", scatter_dimension=0, tiled=True),
    )
    totals = lax.psum(
        (
            owned_query,
            owned_key,
            owned_value,
            owned_out,
            owned_gate,
            owned_up,
            owned_down,
            owned_gain_one,
            owned_gain_two,
        ),
        "replica",
    )
    return (
        output,
        grad_input,
        totals[0],
        totals[1],
        totals[2],
        totals[3],
        totals[4],
        totals[5],
        totals[6],
        totals[7],
        totals[8],
    )


def solution(mesh):
    return jax.shard_map(
        local,
        mesh=mesh,
        in_specs=(
            P(("replica", "group"), None),
            P(("replica", "group"), None),
            P(("replica", "group")),
            P(("replica", "group"), None),
            P("group", None),
            P("group", None),
            P("group", None),
            P(None, "group"),
            P("group", None),
            P("group", None),
            P(None, "group"),
            P("group"),
            P("group"),
        ),
        out_specs=(
            P(("replica", "group"), None),
            P(("replica", "group"), None),
            P("group", None),
            P("group", None),
            P("group", None),
            P(None, "group"),
            P("group", None),
            P("group", None),
            P(None, "group"),
            P("group"),
            P("group"),
        ),
        check_vma=False,
    )
```

profile of v0, /device:TPU:0, one launch (start us, length us, event | category | flops | bytes accessed | tf_op | source)
XLA Modules:
  0.0 516.0 jit_solution(10394361463294998783)
XLA Ops:
  10.2 1.1 fusion.45
  11.3 24.8 %while.31 = (s32[]{:T(128)}, u32[256]{0:T(256)S(1)}, u32[256]{0:T(256)S(1)}, s32[256]{0:T(256)}, s32[]{:T(128)}, /*index=5*/s32[]{:T(128)}, s32[]{}) while((s32[]{:T(128)}, u32[256]{0:T(256)S(1)}, u32[256]{0:T(256)S(1)}, s32[256]{0:T(256)}, s32[]{:T(128)}, /*index=5*/s32[]{:T(128)}, s32[]{}) %tuple.113), condition=%wide.region_2.3_spmd.clone, body=%wide.region_1.2_spmd.clone.sunk | while | flops 5636 | bytes 22117 | solution.py:28
  11.4 2.1 gather_fusion
  14.2 2.0 gather_fusion
  16.9 2.0 gather_fusion
  19.7 2.0 gather_fusion
  22.4 2.0 gather_fusion
  25.2 2.0 gather_fusion
  27.9 2.0 gather_fusion
  30.6 2.0 gather_fusion
  33.4 2.0 gather_fusion
  37.9 8.5 %all-reduce.9 = (bf16[576]{0:T(1024)(128)(2,1)S(1)}, bf16[576]{0:T(1024)(128)(2,1)S(1)}) all-reduce(bf16[576]{0:T(1024)(128)(2,1)S(1)} %dynamic-update-slice.18, bf16[576]{0:T(1024)(128)(2,1)S(1)} %dynamic-update-slice.19), channel_id=1, replica_groups=mesh['replica'=8,'group'=4] {'group'}, use_global_device_ids=true, to_apply=%add.2 | all-reduce | flops 1152 | bytes 4608
  47.3 7.5 %all_gather.38 = bf16[576,192]{1,0:T(8,128)(2,1)S(1)} all-gather(bf16[144,192]{1,0:T(8,128)(2,1)S(1)} %copy-done.55), channel_id=1, replica_groups=mesh['replica'=8,'group'=4] {'group'}, dimensions={0}, use_global_device_ids=true | all-gather | bytes 276480 | tf_op jit(solution)/shard_map/all_gather | solution.py:307
  54.9 8.4 %all_gather.39 = bf16[576,576]{1,0:T(8,128)(2,1)S(1)} all-gather(bf16[144,576]{1,0:T(8,128)(2,1)S(1)} %copy-done.51), channel_id=1, replica_groups=mesh['replica'=8,'group'=4] {'group'}, dimensions={0}, use_global_device_ids=true | all-gather | bytes 829440 | tf_op jit(solution)/shard_map/all_gather | solution.py:306
  65.6 7.7 %all_gather.37 = bf16[576,192]{1,0:T(8,128)(2,1)S(1)} all-gather(bf16[144,192]{1,0:T(8,128)(2,1)S(1)} %copy-done.56), channel_id=1, replica_groups=mesh['replica'=8,'group'=4] {'group'}, dimensions={0}, use_global_device_ids=true | all-gather | bytes 276480 | tf_op jit(solution)/shard_map/all_gather | solution.py:308
  75.9 8.5 %all_gather.40 = bf16[576,576]{0,1:T(8,128)(2,1)S(1)} all-gather(bf16[576,144]{0,1:T(8,128)(2,1)S(1)} %copy-done.52), channel_id=1, replica_groups=mesh['replica'=8,'group'=4] {'group'}, dimensions={1}, use_global_device_ids=true | all-gather | bytes 829440 | tf_op jit(solution)/shard_map/all_gather | solution.py:309
  86.0 3.4 fusion.97
  89.4 3.4 fusion.96
  92.9 4.9 multiply_convert_fusion
  98.4 1.4 copy-done.9
  99.8 1.3 multiply_reduce_fusion
  102.2 1.6 convolution_multiply_fusion.3
  103.8 3.0 copy.79
  107.0 1.8 convolution_convert_fusion
  108.9 1.2 multiply_reduce_fusion.1
  113.6 1.1 convolution_multiply_fusion.8
  114.7 1.3 fusion.20
  116.1 1.7 fusion.30
  119.2 1.1 convolution_multiply_fusion.9
  120.8 1.6 convolution_multiply_fusion.4
  122.5 2.4 convolution_multiply_fusion
  126.0 2.4 convolution_multiply_fusion.1
  129.6 2.5 convolution_multiply_fusion.2
  132.2 3.1 reduce-scatter.22.cloned.1.call-done
  135.3 2.0 copy.80
  137.3 22.6 %reduce-scatter.14.cloned.1.call-done = f32[144,192]{1,0:T(8,128)} async-done(((f32[576,192]{1,0:T(8,128)}), f32[144,192]{1,0:T(8,128)}) %reduce-scatter.14.cloned.1.call-update) | async-done | bytes 110608 | tf_op jit(solution)/shard_map/reduce_scatter | solution.py:353
  159.9 24.6 %reduce-scatter.12.cloned.1.call-done = f32[144,192]{1,0:T(8,128)} async-done(((f32[576,192]{1,0:T(8,128)}), f32[144,192]{1,0:T(8,128)}) %reduce-scatter.12.cloned.1.call-update) | async-done | bytes 110608 | tf_op jit(solution)/shard_map/reduce_scatter | solution.py:352
  184.5 30.3 %reduce-scatter.10.cloned.1.call-done = f32[144,576]{1,0:T(8,128)} async-done(((f32[576,576]{1,0:T(8,128)}), f32[144,576]{1,0:T(8,128)}) %reduce-scatter.10.cloned.1.call-update) | async-done | bytes 331792 | tf_op jit(solution)/shard_map/reduce_scatter | solution.py:351
  214.8 43.0 %reduce-scatter.20.cloned.1.call-done = f32[1536,144]{0,1:T(8,128)} async-done(((f32[1536,576]{0,1:T(8,128)}), f32[1536,144]{0,1:T(8,128)}) %reduce-scatter.20.cloned.1.call-update) | async-done | bytes 884752 | tf_op jit(solution)/shard_map/reduce_scatter | solution.py:357
  257.8 43.2 %reduce-scatter.18.cloned.1.call-done = f32[144,1536]{1,0:T(8,128)} async-done(((f32[576,1536]{1,0:T(8,128)}), f32[144,1536]{1,0:T(8,128)}) %reduce-scatter.18.cloned.1.call-update) | async-done | bytes 884752 | tf_op jit(solution)/shard_map/reduce_scatter | solution.py:356
  301.0 42.9 %reduce-scatter.16.cloned.1.call-done = f32[144,1536]{1,0:T(8,128)} async-done(((f32[576,1536]{1,0:T(8,128)}), f32[144,1536]{1,0:T(8,128)}) %reduce-scatter.16.cloned.1.call-update) | async-done | bytes 884752 | tf_op jit(solution)/shard_map/reduce_scatter | solution.py:355
  345.5 1.4 fusion.44
  346.9 5.9 %all-reduce.8 = (f32[576]{0:T(1024)S(1)}, f32[576]{0:T(1024)S(1)}) all-reduce(f32[576]{0:T(1024)S(1)} %get-tuple-element.255, f32[576]{0:T(1024)S(1)} %get-tuple-element.254), channel_id=9, replica_groups=mesh['replica'=8,'group'=4] {'group'}, use_global_device_ids=true, to_apply=%region_28.29.clone | all-reduce | flops 1152 | bytes 9216
  353.0 23.0 %all-reduce.6 = (f32[144]{0:T(256)}, f32[144]{0:T(256)}) all-reduce(f32[144]{0:T(256)S(1)} %dynamic-slice.49, f32[144]{0:T(256)S(1)} %dynamic-slice.51), channel_id=1, replica_groups=mesh['replica'=8,'group'=4] {'replica'}, use_global_device_ids=true, to_apply=%region_29.30 | all-reduce | flops 288 | bytes 2304 | tf_op jit(solution)/shard_map/psum | solution.py:361
  377.7 1.4 fusion.22
  379.1 122.4 %all-reduce.12.cloned.1.call-done = (f32[144,576]{1,0:T(8,128)}, f32[144,192]{1,0:T(8,128)}, f32[144,192]{1,0:T(8,128)}, f32[576,144]{1,0:T(8,128)}, f32[144,153...) async-done(((f32[144,576]{1,0:T(8,128)}, f32[144,192]{1,0:T(8,128)}, f32[144,192]{1,0:T(8,128)}, f32[576,144]{1,0:T(8,128)}, f32[144,1536]{1,0:T(8,128)}, ...) | async-done | bytes 3538960 | tf_op jit(solution)/shard_map/psum | solution.py:361
  501.5 2.1 copy.65
  503.6 1.8 copy.104
  (279 shorter events, 33.3 us)
Async XLA Ops:
  7.2 78.8 %all-gather.6.cloned.1.call-start = ((), (), s32[]{:S(2)}) async-start(), calls=%async_computation.8 | async-start | bytes 2211840 | tf_op jit(solution)/shard_map/all_gather | solution.py:311
  7.9 81.5 %all-gather.4.cloned.1.call-start = ((), (), s32[]{:S(2)}) async-start(), calls=%async_computation.7 | async-start | bytes 2211840 | tf_op jit(solution)/shard_map/all_gather | solution.py:310
  8.7 84.2 %all-gather.8.cloned.1.call-start = ((), (), s32[]{:S(2)}) async-start(), calls=%async_computation.9 | async-start | bytes 2211840 | tf_op jit(solution)/shard_map/all_gather | solution.py:312
  9.4 125.9 %reduce-scatter.22.cloned.1.call-start = ((), (), s32[]{:S(2)}) async-start(), calls=%async_computation.16 | async-start | bytes 1843200
  10.1 36.3 %copy-start.64 = (pred[256]{0:T(512)(128)(4,1)}, pred[256]{0:T(512)(128)(4,1)S(1)}, u32[]{:S(2)}) copy-start(pred[256]{0:T(512)(128)(4,1)S(1)} %iota_compare_fusion.2) | copy-start | bytes 772
  11.2 62.0 %copy-start.59 = (f32[256]{0:T(256)}, f32[256]{0:T(256)S(1)}, u32[]{:S(2)}) copy-start(f32[256]{0:T(256)S(1)} %add_rsqrt_fusion.1) | copy-start | bytes 3076
  11.2 24.9 %copy-start.67 = (u32[32]{0:T(128)S(1)}, u32[32]{0:T(128)}, u32[]{:S(2)}) copy-start(u32[32]{0:T(128)} %constant.211) | copy-start | bytes 388
  11.3 26.2 %copy-start.68 = (bf16[144]{0:T(256)(128)(2,1)S(1)}, bf16[144]{0:T(256)(128)(2,1)}, u32[]{:S(2)}) copy-start(bf16[144]{0:T(256)(128)(2,1)} %param.38) | copy-start | bytes 868
  11.3 26.4 %copy-start.69 = (bf16[144]{0:T(256)(128)(2,1)S(1)}, bf16[144]{0:T(256)(128)(2,1)}, u32[]{:S(2)}) copy-start(bf16[144]{0:T(256)(128)(2,1)} %param.39) | copy-start | bytes 868
  11.3 36.0 %copy-start.55 = (bf16[144,192]{1,0:T(8,128)(2,1)S(1)}, bf16[144,192]{1,0:T(8,128)(2,1)}, u32[]{:S(2)}) copy-start(bf16[144,192]{1,0:T(8,128)(2,1)} %param.32) | copy-start | bytes 165892
  11.3 43.6 %copy-start.51 = (bf16[144,576]{1,0:T(8,128)(2,1)S(1)}, bf16[144,576]{1,0:T(8,128)(2,1)}, u32[]{:S(2)}) copy-start(bf16[144,576]{1,0:T(8,128)(2,1)} %param.31) | copy-start | bytes 497668
  11.3 52.0 %copy-start = (bf16[256,576]{0,1:T(8,128)(2,1)S(1)}, bf16[256,576]{0,1:T(8,128)(2,1)}, u32[]{:S(2)}) copy-start(bf16[256,576]{0,1:T(8,128)(2,1)} %param.27) | copy-start | bytes 884740
  54.9 9.7 %copy-start.33 = (bf16[576,192]{1,0:T(8,128)(2,1)}, bf16[576,192]{1,0:T(8,128)(2,1)S(1)}, u32[]{:S(2)}) copy-start(bf16[576,192]{1,0:T(8,128)(2,1)S(1)} %all_gather.38) | copy-start | bytes 663556
  64.6 9.8 %copy-start.26 = (bf16[256,3,32]{0,2,1:T(8,128)(2,1)}, bf16[256,3,32]{0,2,1:T(8,128)(2,1)S(1)}, u32[]{:S(2)}) copy-start(bf16[256,3,32]{0,2,1:T(8,128)(2,1)S(1)} %get-tuple-element.235) | copy-start | bytes 147460
  64.6 9.8 %copy-start.28 = (bf16[256,3,32]{0,2,1:T(8,128)(2,1)}, bf16[256,3,32]{0,2,1:T(8,128)(2,1)S(1)}, u32[]{:S(2)}) copy-start(bf16[256,3,32]{0,2,1:T(8,128)(2,1)S(1)} %get-tuple-element.236) | copy-start | bytes 147460
  64.7 9.7 %copy-start.3 = (bf16[256,9,32]{0,2,1:T(8,128)(2,1)}, bf16[256,9,32]{0,2,1:T(8,128)(2,1)S(1)}, u32[]{:S(2)}) copy-start(bf16[256,9,32]{0,2,1:T(8,128)(2,1)S(1)} %get-tuple-element.231) | copy-start | bytes 442372
  64.7 9.7 %copy-start.6 = (bf16[256,9,32]{0,2,1:T(8,128)(2,1)}, bf16[256,9,32]{0,2,1:T(8,128)(2,1)S(1)}, u32[]{:S(2)}) copy-start(bf16[256,9,32]{0,2,1:T(8,128)(2,1)S(1)} %get-tuple-element.232) | copy-start | bytes 442372
  74.9 9.5 %copy-start.57 = (f32[3,256]{1,0:T(4,128)}, f32[3,256]{1,0:T(4,128)S(1)}, u32[]{:S(2)}) copy-start(f32[3,256]{1,0:T(4,128)S(1)} %log_add_fusion.1) | copy-start | bytes 9220
  75.9 9.4 %copy-start.24 = (bf16[256,3,3,64]{0,3,2,1:T(8,128)(2,1)}, bf16[256,3,3,64]{0,3,2,1:T(8,128)(2,1)S(1)}, u32[]{:S(2)}) copy-start(bf16[256,3,3,64]{0,3,2,1:T(8,128)(2,1)S(1)} %pad_maximum_fusion.1) | copy-start | bytes 884740
  92.9 4.9 copy-start.10
  97.7 3.4 copy-start.19
  97.8 3.4 copy-start.22
  97.8 2.0 copy-start.9
  97.8 2.0 copy-start.62
  106.8 53.1 %reduce-scatter.14.cloned.1.call-start = ((), (), s32[]{:S(2)}) async-start(), calls=%async_computation.12 | async-start | bytes 737280 | tf_op jit(solution)/shard_map/reduce_scatter | solution.py:353
  107.0 3.7 copy-start.50
  107.0 4.0 copy-start.4
  107.0 4.0 copy-start.7
  108.9 3.4 copy-start.14
  112.2 2.4 copy-start.37
  112.6 3.5 copy-start.5
  112.6 3.5 copy-start.8
  114.7 4.1 copy-start.16
  114.7 4.1 copy-start.27
  114.7 4.1 copy-start.29
  114.7 4.3 copy-start.18
  116.0 68.5 %reduce-scatter.12.cloned.1.call-start = ((), (), s32[]{:S(2)}) async-start(), calls=%async_computation.11 | async-start | bytes 737280 | tf_op jit(solution)/shard_map/reduce_scatter | solution.py:352
  120.4 94.4 %reduce-scatter.10.cloned.1.call-start = ((), (), s32[]{:S(2)}) async-start(), calls=%async_computation.10 | async-start | bytes 1843200 | tf_op jit(solution)/shard_map/reduce_scatter | solution.py:351
  122.4 135.4 %reduce-scatter.20.cloned.1.call-start = ((), (), s32[]{:S(2)}) async-start(), calls=%async_computation.15 | async-start | bytes 4423680 | tf_op jit(solution)/shard_map/reduce_scatter | solution.py:357
  124.9 176.1 %reduce-scatter.18.cloned.1.call-start = ((), (), s32[]{:S(2)}) async-start(), calls=%async_computation.14 | async-start | bytes 4423680 | tf_op jit(solution)/shard_map/reduce_scatter | solution.py:356
  128.5 215.4 %reduce-scatter.16.cloned.1.call-start = ((), (), s32[]{:S(2)}) async-start(), calls=%async_computation.13 | async-start | bytes 4423680 | tf_op jit(solution)/shard_map/reduce_scatter | solution.py:355
  132.1 369.4 %all-reduce.12.cloned.1.call-start = ((), (), s32[]{:S(2)}) async-start(), calls=%async_computation.17 | async-start | bytes 7815168 | tf_op jit(solution)/shard_map/psum | solution.py:361
  345.1 30.9 %copy-start.2 = (f32[256,576]{0,1:T(8,128)S(1)}, f32[256,576]{0,1:T(8,128)}, u32[]{:S(2)}) copy-start(f32[256,576]{0,1:T(8,128)} %copy-done.1) | copy-start | bytes 1769476
  501.5 3.9 copy-start.54
  501.5 4.6 copy-start.53
  501.5 5.3 %copy-start.44 = (f32[144,1536]{1,0:T(8,128)S(1)}, f32[144,1536]{1,0:T(8,128)}, u32[]{:S(2)}) copy-start(f32[144,1536]{1,0:T(8,128)} %get-tuple-element.312) | copy-start | bytes 2654212
  503.6 4.1 copy-start.43
  506.7 1.8 copy-start.42
  (33 other events, 39.2 us)
Sparse Core Ops, SparseCore 0:
  9.6 23.4 all-gather.5
  34.6 22.3 all-gather.3
  58.6 22.4 all-gather.7
  106.9 28.3 reduce-scatter.21
  137.8 22.0 reduce-scatter.13
  162.4 22.0 reduce-scatter.11
  187.2 27.5 reduce-scatter.9
  217.4 40.4 reduce-scatter.19
  260.6 40.4 reduce-scatter.17
  303.4 40.4 reduce-scatter.15
  349.7 151.7 all-reduce.11
where the time goes:
time: 517 us; the launch traced here: 516 us
  waiting for transfers between devices  334 us (65%)
  blocking collectives  69.5 us (13%)
  local copies, waits for them, and re-layouts  40.9 us (8%)
  matrix products  40.5 us (8%)
  between operations  16.9 us (3%)
  other arithmetic  12.9 us (2%)
    psum x1, waiting for transfers between devices, local(): lax.psum((owned_query, owned_key, owned_value, owned_out, owned_gate, own...  122 us
    reduce_scatter x1, waiting for transfers between devices, local(): lax.psum_scatter(grad_up_w, 'group', scatter_dimension=0, tiled=True)  43.2 us
    reduce_scatter x1, waiting for transfers between devices, local(): lax.psum_scatter(grad_down_w, 'group', scatter_dimension=1, tiled=True)  43 us
    reduce_scatter x1, waiting for transfers between devices, local(): lax.psum_scatter(grad_gate_w, 'group', scatter_dimension=0, tiled=True)  42.9 us
    dot_general x21, matrix products, matmul(): return jnp.dot(left_op, right_op, preferred_element_type=jnp.float32)  33.4 us
    reduce_scatter x1, waiting for transfers between devices, local(): lax.psum_scatter(grad_query_w, 'group', scatter_dimension=0, tiled=True)  30.3 us
    reduce_scatter x1, waiting for transfers between devices, local(): lax.psum_scatter(grad_key_w, 'group', scatter_dimension=0, tiled=True)  24.6 us
    psum x1, blocking collectives, local(): lax.psum((owned_query, owned_key, owned_value, owned_out, owned_gate, own...  23 us
  transfers between devices with their start and end apart: 11, of which 8 were waited for; matrix products, arithmetic and copies ran while one was open for 13% of the time, Pallas kernels for 0%

commit v1 on v0

v1 whole, which is shorter than its diff:
```python
import math

import jax
import jax.numpy as jnp
from jax import lax
from jax.experimental import pallas as pl
from jax.experimental.pallas import tpu as pltpu
from jax.sharding import PartitionSpec as P

HEADS = 9
KV_HEADS = 3
HEAD = 64
WIDTH = 576
FF = 1536
QKV = 960
CH = 256
NCH = 25
FF_CH = 6
G_OUT = 18
G_QKV = 20
G_TAIL = 24
W_TAIL = 0
W_QKV = 1
W_OUT = 5
W_FF = 7
LAG = 2

norm_eps = 1e-05
rope_base = 100000.0
masked_value = -1e30
MESH = pl.DeviceIdType.MESH
f32 = jnp.float32
bf16 = jnp.bfloat16


def nn(a, b):
    return lax.dot_general(a, b, (((1,), (0,)), ((), ())), preferred_element_type=f32)


def nt(a, b):
    return lax.dot_general(a, b, (((1,), (1,)), ((), ())), preferred_element_type=f32)


def tn(a, b):
    return lax.dot_general(a, b, (((0,), (0,)), ((), ())), preferred_element_type=f32)


class Where:
    def __init__(self, shard, chain):
        self.rep = lax.axis_index("replica")
        self.grp = lax.axis_index("group")
        self.core = lax.rem(self.grp, 2)
        self.y = lax.div(self.grp, 2)
        self.xp = lax.rem(self.rep, 2)
        self.q = lax.div(self.rep, 2)
        self.core_peer = (self.rep, self.y * 2 + 1 - self.core)
        self.y_peer = (self.rep, (1 - self.y) * 2 + self.core)
        self.x_peer = (self.rep + 1 - 2 * self.xp, self.grp)
        self.left = (self.rep - 2, self.grp)
        self.right = (self.rep + 2, self.grp)
        self.shard = shard
        self.chain = chain

    def rows(self, y, core):
        return pl.ds(pl.multiple_of((y * 2 + core) * self.shard, 16), self.shard)


def enter(w, use_chain):
    barrier = pltpu.get_barrier_semaphore()
    for peer in (w.core_peer, w.y_peer, w.x_peer):
        pl.semaphore_signal(barrier, inc=1, device_id=peer, device_id_type=MESH)
    if use_chain:
        for step in (1, w.chain - 1):
            peer = (lax.rem(w.q + step, w.chain) * 2 + w.xp, w.grp)
            pl.semaphore_signal(barrier, inc=1, device_id=peer, device_id_type=MESH)
    pl.semaphore_wait(barrier, 5 if use_chain else 3)


def remote(src, dst, send, recv, peer):
    return pltpu.make_async_remote_copy(
        src_ref=src, dst_ref=dst, send_sem=send, recv_sem=recv, device_id=peer, device_id_type=MESH
    )


class Gather:
    def __init__(self, w, own, full, sems):
        self.w, self.own, self.full = w, own, full
        self.s1, self.r1, self.s2, self.r2, self.sy, self.sx, self.ryx = sems
        self.mine = w.grp
        self.other = (1 - w.y) * 2 + w.core

    def core_own(self, k):
        return remote(
            self.own.at[k],
            self.full.at[self.mine, k],
            self.s1.at[k],
            self.r1.at[k],
            self.w.core_peer,
        )

    def y_own(self, k):
        return remote(
            self.own.at[k],
            self.full.at[self.mine, k],
            self.sy.at[k],
            self.ryx.at[k],
            self.w.y_peer,
        )

    def x_fwd(self, k):
        block = self.full.at[self.other, k]
        return remote(block, block, self.sx.at[k], self.ryx.at[k], self.w.x_peer)

    def core_fwd(self, k):
        block = self.full.at[self.other, k]
        return remote(block, block, self.s2.at[k], self.r2.at[k], self.w.core_peer)

    def start(self):
        @pl.loop(0, NCH)
        def _(k):
            @pl.when(lax.rem(k, 2) == self.w.xp)
            def _():
                self.y_own(k).start()

            self.core_own(k).start()
            self.full[self.mine, k] = self.own[k]

    def relay(self, j):
        near = 2 * j + self.w.xp
        far = 2 * (j - LAG) + 1 - self.w.xp

        @pl.when(near < NCH)
        def _():
            self.y_own(near).wait_recv()
            self.x_fwd(near).start()
            self.core_fwd(near).start()

        @pl.when((far >= 0) & (far < NCH))
        def _():
            self.x_fwd(far).wait_recv()
            self.core_fwd(far).start()

    def ready(self, k):
        self.core_own(k).wait_recv()
        self.core_fwd(k).wait_recv()

    def drain(self):
        @pl.loop(0, NCH)
        def _(k):
            self.core_own(k).wait_send()
            self.core_fwd(k).wait_send()

            @pl.when(lax.rem(k, 2) == self.w.xp)
            def _():
                self.y_own(k).wait_send()
                self.x_fwd(k).wait_send()


class Reduce:
    def __init__(self, w, grads, total, bufs, sems, scale):
        self.w, self.g, self.o, self.scale = w, grads, total, scale
        self.ra, self.sb, self.rb, self.tc, self.rc, self.pr, self.rl, self.pq, self.rr = bufs
        (
            self.sa,
            self.rsa,
            self.ssb,
            self.rsb,
            self.ssc,
            self.rsc,
            self.ssr,
            self.rsr,
            self.ssl,
            self.rsl,
        ) = sems

    def core_send(self, side, k):
        return remote(
            self.g.at[k, self.w.rows(side, 1 - self.w.core), :],
            self.ra.at[side, k],
            self.sa.at[side, k],
            self.rsa.at[side, k],
            self.w.core_peer,
        )

    def y_send(self, k):
        return remote(
            self.sb.at[k], self.rb.at[k], self.ssb.at[k], self.rsb.at[k], self.w.y_peer
        )

    def x_send(self, k):
        return remote(
            self.tc.at[k], self.rc.at[k], self.ssc.at[k], self.rsc.at[k], self.w.x_peer
        )

    def right_send(self, k):
        return remote(
            self.pr.at[k], self.rl.at[k], self.ssr.at[k], self.rsr.at[k], self.w.right
        )

    def left_send(self, k):
        return remote(self.pq.at[k], self.rr.at[k], self.ssl.at[k], self.rsl.at[k], self.w.left)

    def first(self, k):
        self.core_send(0, k).start()
        self.core_send(1, k).start()

    def steps(self):
        return NCH + LAG * 2 + LAG * (self.w.chain - 1)

    def step(self, t):
        w = self.w

        def at(k, body):
            pl.when((k >= 0) & (k < NCH))(lambda: body(k))

        def stage_y(k):
            self.core_send(0, k).wait_recv()
            self.core_send(1, k).wait_recv()
            away = self.g[k, w.rows(1 - w.y, w.core), :].astype(f32) + self.ra[1 - w.y, k].astype(
                f32
            )
            self.sb[k] = away.astype(bf16)
            self.y_send(k).start()
            self.o[k] = self.g[k, w.rows(w.y, w.core), :].astype(f32) + self.ra[w.y, k].astype(f32)

        def stage_x(k):
            self.y_send(k).wait_recv()
            total = self.o[k] + self.rb[k].astype(f32)
            self.tc[k] = total.astype(bf16)
            self.x_send(k).start()

        def stage_pair(k):
            self.x_send(k).wait_recv()
            self.o[k] = self.tc[k].astype(f32) + self.rc[k].astype(f32)

        def stage_right(k):
            @pl.when(w.q > 0)
            def _():
                self.right_send(k).wait_recv()

            @pl.when((w.q > 0) & (w.q < w.chain - 1))
            def _():
                self.pr[k] = (self.o[k] + self.rl[k].astype(f32)).astype(bf16)

            @pl.when(w.q == 0)
            def _():
                self.pr[k] = self.o[k].astype(bf16)

            @pl.when(w.q < w.chain - 1)
            def _():
                self.right_send(k).start()

        def stage_left(k):
            @pl.when(w.q < w.chain - 1)
            def _():
                self.left_send(k).wait_recv()

            @pl.when((w.q > 0) & (w.q < w.chain - 1))
            def _():
                self.pq[k] = (self.o[k] + self.rr[k].astype(f32)).astype(bf16)

            @pl.when(w.q == w.chain - 1)
            def _():
                self.pq[k] = self.o[k].astype(bf16)

            @pl.when(w.q > 0)
            def _():
                self.left_send(k).start()

        def stage_last(k):
            @pl.when(w.q > 0)
            def _():
                self.o[k] = self.o[k] + self.rl[k].astype(f32)

            @pl.when(w.q < w.chain - 1)
            def _():
                self.o[k] = self.o[k] + self.rr[k].astype(f32)

            self.o[k] = self.o[k] * self.scale

        at(t, stage_y)
        at(t - LAG, stage_x)
        at(t - 2 * LAG, stage_pair)
        at(t - 2 * LAG - LAG * w.q, stage_right)
        at(t - 2 * LAG - LAG * (w.chain - 1 - w.q), stage_left)
        at(t - 2 * LAG - LAG * (w.chain - 1), stage_last)

    def drain(self):
        w = self.w

        @pl.loop(0, NCH)
        def _(k):
            self.core_send(0, k).wait_send()
            self.core_send(1, k).wait_send()
            self.y_send(k).wait_send()
            self.x_send(k).wait_send()

            @pl.when(w.q < w.chain - 1)
            def _():
                self.right_send(k).wait_send()

            @pl.when(w.q > 0)
            def _():
                self.left_send(k).wait_send()


def rope(values, cosine, sine, sign):
    lane = lax.broadcasted_iota(jnp.int32, values.shape, 1)
    low = lax.rem(lane, HEAD) < HEAD // 2
    swapped = jnp.where(
        low, pltpu.roll(values, 128 - HEAD // 2, 1), pltpu.roll(values, HEAD // 2, 1)
    )
    return values * cosine + swapped * jnp.where(low, -sign * sine, sign * sine)


def compute(
    wait_w,
    give_g,
    x_ref,
    cot_ref,
    seg_row,
    seg_col,
    live_ref,
    w_ref,
    out_ref,
    gin_ref,
    g_ref,
    raw,
    qkv,
    attn,
    gattn,
    probs,
    gqkv,
    mids,
    mixes,
):
    rows = x_ref.shape[0]

    def wt(k):
        return w_ref[:, k].reshape(WIDTH, CH)

    live = live_ref[0, 0]
    pos_row = lax.broadcasted_iota(jnp.int32, (rows, rows), 1)
    pos_col = lax.broadcasted_iota(jnp.int32, (rows, rows), 0)
    keys, queries = seg_row[...], seg_col[...]
    allowed = (
        (keys == queries)
        & (pos_row <= pos_col)
        & ((pos_row < live) | (pos_row == pos_col))
    )
    first = jnp.sum(jnp.where(keys < queries, 1.0, 0.0).astype(f32), axis=1, keepdims=True)
    lane = lax.broadcasted_iota(jnp.int32, (rows, 128), 1)
    index = lax.broadcasted_iota(jnp.int32, (rows, 128), 0).astype(f32)
    freq = jnp.exp(
        lax.rem(lane, HEAD // 2).astype(f32) * (-2.0 * math.log(rope_base) / HEAD)
    )
    angle = (index - first) * freq
    cosine, sine = jnp.cos(angle), jnp.sin(angle)

    xf = x_ref[...].astype(f32)
    r1 = lax.rsqrt(jnp.mean(xf * xf, axis=-1, keepdims=True) + norm_eps)
    n1 = xf * r1
    wait_w(W_TAIL)
    gains = wt(W_TAIL)[:, 128:256].astype(f32).T
    gain1, gain2 = gains[0:1, :], gains[64:65, :]
    h1 = (n1 * gain1).astype(bf16)
    for j in range(4):
        wait_w(W_QKV + j)
        raw[:, j * CH : (j + 1) * CH] = nn(h1, wt(W_QKV + j))
    for j in range(6):
        qkv[:, j * 128 : (j + 1) * 128] = rope(
            raw[:, j * 128 : (j + 1) * 128], cosine, sine, 1.0
        ).astype(bf16)
    qkv[:, 768:1024] = raw[:, 768:1024].astype(bf16)

    score_scale = HEAD ** (-0.5)

    def head(ref, at):
        return ref[:, at * HEAD : (at + 1) * HEAD]

    for h in range(HEADS):
        kv = h // 3
        s = nt(head(qkv, h), head(qkv, HEADS + kv)) * score_scale
        s = jnp.where(allowed, s, masked_value)
        e = jnp.exp(s - jnp.max(s, axis=1, keepdims=True))
        p = e * (1.0 / jnp.sum(e, axis=1, keepdims=True))
        probs[h] = p
        attn[:, h * HEAD : (h + 1) * HEAD] = nn(
            p.astype(bf16), head(qkv, HEADS + KV_HEADS + kv)
        ).astype(bf16)

    wait_w(W_OUT)
    wait_w(W_OUT + 1)
    mid = (
        xf
        + nt(attn[:, 0:256], wt(W_OUT))
        + nt(attn[:, 256:512], wt(W_OUT + 1))
        + nt(attn[:, 512:576], wt(W_TAIL)[:, 0:64])
    )
    r2 = lax.rsqrt(jnp.mean(mid * mid, axis=-1, keepdims=True) + norm_eps)
    n2 = mid * r2
    h2 = (n2 * gain2).astype(bf16)
    h2t = h2.T
    live_rows = lax.broadcasted_iota(jnp.int32, (rows, 1), 0) < live
    cot_f = jnp.where(live_rows, cot_ref[...].astype(f32), 0.0)
    cot = cot_f.astype(bf16)
    cott = cot.T

    mids[...] = mid
    gh2 = jnp.zeros((rows, WIDTH), f32)
    for j in range(FF_CH):
        kd, kg, ku = W_FF + 3 * j, W_FF + 3 * j + 1, W_FF + 3 * j + 2
        wait_w(kd)
        wait_w(kg)
        wait_w(ku)
        gate = nn(h2, wt(kg))
        up = nn(h2, wt(ku))
        gm = nn(cot, wt(kd))
        sig = 1.0 / (1.0 + jnp.exp(-gate))
        silu = gate * sig
        mixed = (silu * up).astype(bf16)
        mixes[:, j * CH : (j + 1) * CH] = mixed
        g_ref[3 * j] = nn(cott, mixed).astype(bf16)
        give_g(3 * j)
        ggate = (gm * up * (sig * (1.0 + gate * (1.0 - sig)))).astype(bf16)
        gup = (gm * silu).astype(bf16)
        g_ref[3 * j + 1] = nn(h2t, ggate).astype(bf16)
        give_g(3 * j + 1)
        g_ref[3 * j + 2] = nn(h2t, gup).astype(bf16)
        give_g(3 * j + 2)
        gh2 = gh2 + nt(ggate, wt(kg)) + nt(gup, wt(ku))

    gn = gh2 * gain2
    gmid = cot_f + r2 * (gn - n2 * jnp.mean(gn * n2, axis=-1, keepdims=True))
    ggain2 = jnp.sum(gh2 * n2, axis=0, keepdims=True)
    gmid_bf = gmid.astype(bf16)
    gmidt = gmid_bf.T
    for j in range(2):
        g_ref[G_OUT + j] = nn(gmidt, attn[:, j * CH : (j + 1) * CH]).astype(bf16)
        give_g(G_OUT + j)
        gattn[:, j * CH : (j + 1) * CH] = nn(gmid_bf, wt(W_OUT + j)).astype(bf16)
    gattn[:, 512:576] = nn(gmid_bf, wt(W_TAIL)[:, 0:64]).astype(bf16)
    tail_grad = nn(gmidt, attn[:, 512:640]).astype(bf16)

    for kv in range(KV_HEADS):
        gk = jnp.zeros((rows, HEAD), f32)
        gv = jnp.zeros((rows, HEAD), f32)
        for h in range(3 * kv, 3 * kv + 3):
            ga = head(gattn, h)
            p = probs[h]
            delta = jnp.sum(
                ga.astype(f32) * head(attn, h).astype(f32), axis=1, keepdims=True
            )
            gp = nt(ga, head(qkv, HEADS + KV_HEADS + kv))
            gs = (p * (gp - delta) * score_scale).astype(bf16)
            raw[:, h * HEAD : (h + 1) * HEAD] = nn(gs, head(qkv, HEADS + kv))
            gk = gk + tn(gs, head(qkv, h))
            gv = gv + tn(p.astype(bf16), ga)
        raw[:, (HEADS + kv) * HEAD : (HEADS + kv + 1) * HEAD] = gk
        at = HEADS + KV_HEADS + kv
        raw[:, at * HEAD : (at + 1) * HEAD] = gv
    raw[:, QKV:1024] = jnp.zeros((rows, 1024 - QKV), f32)
    for j in range(6):
        gqkv[:, j * 128 : (j + 1) * 128] = rope(
            raw[:, j * 128 : (j + 1) * 128], cosine, sine, -1.0
        ).astype(bf16)
    gqkv[:, 768:1024] = raw[:, 768:1024].astype(bf16)
    h1t = h1.T
    gh1 = jnp.zeros((rows, WIDTH), f32)
    for j in range(4):
        block = gqkv[:, j * CH : (j + 1) * CH]
        g_ref[G_QKV + j] = nn(h1t, block).astype(bf16)
        give_g(G_QKV + j)
        gh1 = gh1 + nt(block, wt(W_QKV + j))
    gm1 = gh1 * gain1
    gin_ref[...] = gmid + r1 * (gm1 - n1 * jnp.mean(gm1 * n1, axis=-1, keepdims=True))
    ggain1 = jnp.sum(gh1 * n1, axis=0, keepdims=True)
    which = lax.broadcasted_iota(jnp.int32, (128, WIDTH), 0) < 64
    gain_grads = jnp.where(which, ggain1, ggain2).T
    g_ref[G_TAIL, :, 0:128] = tail_grad
    g_ref[G_TAIL, :, 128:256] = gain_grads.astype(bf16)
    give_g(G_TAIL)
    for j in range(FF_CH):
        mids[...] += nt(mixes[:, j * CH : (j + 1) * CH], wt(W_FF + 3 * j))
    out_ref[...] = jnp.where(live_rows, mids[...], 0.0).astype(bf16)


def compute_scratch(rows):
    return [
        pltpu.VMEM((rows, 1024), f32),
        pltpu.VMEM((rows, 1024), bf16),
        pltpu.VMEM((rows, 640), bf16),
        pltpu.VMEM((rows, 640), bf16),
        pltpu.VMEM((HEADS, rows, rows), f32),
        pltpu.VMEM((rows, 1024), bf16),
        pltpu.VMEM((rows, WIDTH), f32),
        pltpu.VMEM((rows, FF), bf16),
    ]


def dma(*shape):
    return pltpu.SemaphoreType.DMA(shape)


def gather_kernel(chain, own, full, *sems):
    w = Where(own.shape[1], chain)
    enter(w, False)
    gather = Gather(w, own, full, sems)
    gather.start()

    @pl.loop(0, (NCH + 1) // 2 + LAG)
    def _(j):
        gather.relay(j)

    @pl.loop(0, NCH)
    def _(k):
        gather.ready(k)

    gather.drain()


def reduce_kernel(chain, scale, grads, total, *rest):
    w = Where(total.shape[1], chain)
    enter(w, True)
    red = Reduce(w, grads, total, rest[:9], rest[9:], scale)

    @pl.loop(0, NCH)
    def _(k):
        red.first(k)

    @pl.loop(0, red.steps())
    def _(t):
        red.step(t)

    red.drain()


def compute_kernel(x, cot, srow, scol, live, w, out, gin, g, *scratch):
    scratch[2][:, 512:640] = jnp.zeros((x.shape[0], 128), bf16)
    compute(
        lambda k: None, lambda k: None, x, cot, srow, scol, live, w, out, gin, g, *scratch
    )


def pack(w_query, w_key, w_value, w_out, w_gate, w_up, w_down, norm_attn, norm_ffn):
    shard = w_query.shape[0]

    def split(matrix):
        return jnp.transpose(matrix.reshape(shard, -1, CH), (1, 0, 2))

    out_t = w_out.T
    wide = jnp.concatenate(
        [w_query, w_key, w_value, jnp.zeros((shard, 1024 - QKV), bf16)], axis=1
    )
    tail = jnp.concatenate(
        [
            out_t[:, 512:576],
            jnp.zeros((shard, 64), bf16),
            jnp.broadcast_to(norm_attn[:, None], (shard, 64)),
            jnp.broadcast_to(norm_ffn[:, None], (shard, 64)),
        ],
        axis=1,
    )
    ff = jnp.stack([split(w_down.T), split(w_gate), split(w_up)], axis=1)
    return jnp.concatenate(
        [tail[None], split(wide), split(out_t[:, :512]), ff.reshape(3 * FF_CH, shard, CH)],
        axis=0,
    )


def unpack(total):
    shard = total.shape[1]

    def join(chunks):
        return jnp.transpose(chunks, (1, 0, 2)).reshape(shard, -1)

    ff = total[: 3 * FF_CH].reshape(FF_CH, 3, shard, CH)
    qkv = join(total[G_QKV : G_QKV + 4])
    tail = total[G_TAIL]
    out_t = jnp.concatenate([join(total[G_OUT : G_OUT + 2]), tail[:, :64]], axis=1)
    return (
        qkv[:, :576],
        qkv[:, 576:768],
        qkv[:, 768:960],
        out_t.T,
        join(ff[:, 1]),
        join(ff[:, 2]),
        join(ff[:, 0]).T,
        tail[:, 128],
        tail[:, 192],
    )


def local(inputs, segment_ids, live_counts, cotangent, *weights):
    rows = inputs.shape[0]
    chain = lax.axis_size("replica") // 2
    token_total = rows * lax.axis_size("replica") * lax.axis_size("group")
    scale = float(token_total) ** (-0.5)
    own = pack(*weights)
    shard = own.shape[1]
    vmem = pl.BlockSpec(memory_space=pltpu.VMEM)

    full = pl.pallas_call(
        lambda *refs: gather_kernel(chain, *refs),
        out_shape=jax.ShapeDtypeStruct((4, NCH, shard, CH), bf16),
        in_specs=[vmem],
        out_specs=vmem,
        scratch_shapes=[dma(NCH)] * 7,
        compiler_params=pltpu.CompilerParams(
            collective_id=0, has_side_effects=True, vmem_limit_bytes=60 << 20
        ),
        name="gather",
    )(own)
    output, grad_input, grads = pl.pallas_call(
        compute_kernel,
        out_shape=(
            jax.ShapeDtypeStruct((rows, WIDTH), bf16),
            jax.ShapeDtypeStruct((rows, WIDTH), f32),
            jax.ShapeDtypeStruct((NCH, WIDTH, CH), bf16),
        ),
        in_specs=[vmem] * 4 + [pl.BlockSpec(memory_space=pltpu.SMEM), vmem],
        out_specs=(
            pl.BlockSpec((rows, WIDTH), lambda: (0, 0)),
            pl.BlockSpec((rows, WIDTH), lambda: (0, 0)),
            vmem,
        ),
        scratch_shapes=compute_scratch(rows),
        compiler_params=pltpu.CompilerParams(vmem_limit_bytes=60 << 20),
        name="layer",
    )(
        inputs,
        cotangent,
        segment_ids,
        segment_ids.reshape(rows, 1),
        live_counts.reshape(1, 1),
        full,
    )
    buf = pltpu.VMEM((NCH, shard, CH), bf16)
    total = pl.pallas_call(
        lambda *refs: reduce_kernel(chain, scale, *refs),
        out_shape=jax.ShapeDtypeStruct((NCH, shard, CH), f32),
        in_specs=[vmem],
        out_specs=vmem,
        scratch_shapes=[pltpu.VMEM((2, NCH, shard, CH), bf16)]
        + [buf] * 8
        + [dma(2, NCH)] * 2
        + [dma(NCH)] * 8,
        compiler_params=pltpu.CompilerParams(
            collective_id=1, has_side_effects=True, vmem_limit_bytes=60 << 20
        ),
        name="reduce",
    )(grads)
    return (output, grad_input) + unpack(total)


def solution(mesh):
    rows = P(("replica", "group"), None)
    weight = [P("group", None)] * 3 + [P(None, "group")] + [P("group", None)] * 2
    weight = weight + [P(None, "group"), P("group"), P("group")]
    return jax.shard_map(
        local,
        mesh=mesh,
        in_specs=(rows, rows, P(("replica", "group")), rows, *weight),
        out_specs=(rows, rows, *weight),
        check_vma=False,
    )
```

time: 517 us -> 162 us (0.31)
  waiting for transfers between devices: 334 us -> 0 us
  Pallas kernels: 0 us -> 133 us
  blocking collectives: 69.5 us -> 0 us
  matrix products: 40.5 us -> 0 us
  local copies, waits for them, and re-layouts: 40.9 us -> 22.5 us
  between operations: 16.9 us -> 1.59 us
  other arithmetic: 12.9 us -> 3.94 us
    reduce_scatter x6 -> x0, waiting for transfers between devices: 207 us -> none  [the longest x1 43.2 us: local(): lax.psum_scatter(grad_up_w, 'group', scatter_dimension=0, tiled=True)]
    pallas_call x0 -> x3, Pallas kernels: none -> 133 us  [the longest x1 75.7 us: local(): pl.pallas_call(lambda *refs: reduce_kernel(chain, scale, *refs), out_shap...]
    psum x1 -> x0, waiting for transfers between devices: 122 us -> none  [local(): lax.psum((owned_query, owned_key, owned_value, owned_out, owned_gate, own...]
    dot_general x39 -> x0, matrix products: 40.5 us -> none  [the longest x21 33.4 us: matmul(): return jnp.dot(left_op, right_op, preferred_element_type=jnp.float32)]
    all_gather x4 -> x0, blocking collectives: 32.1 us -> none  [the longest x1 8.48 us: local(): lax.all_gather(w_out, 'group', axis=1, tiled=True)]
    psum x1 -> x0, blocking collectives: 23 us -> none  [local(): lax.psum((owned_query, owned_key, owned_value, owned_out, owned_gate, own...]
    gather x9 -> x0, local copies, waits for them, and re-layouts: 18 us -> none  [rope_tables(): seg_first = jnp.searchsorted(segment_row, segment_row, side='left')]
    unnamed x2 -> x0, blocking collectives: 14.4 us -> none
  transfers between devices with their start and end apart: 11 -> 0, of which waited for: 8 -> 0; matrix products, arithmetic and copies ran while one was open for 13% -> 0% of each run, Pallas kernels for 0% -> 0%
where the time goes in v1:
time: 162 us; the launch traced here: 161 us
  Pallas kernels  133 us (82%)
  local copies, waits for them, and re-layouts  22.5 us (14%)
  other arithmetic  3.94 us (2%)
    pallas_call x1, Pallas kernels, local(): pl.pallas_call(lambda *refs: reduce_kernel(chain, scale, *refs), out_shap...  75.7 us
    pallas_call x1, Pallas kernels, local(): pl.pallas_call(lambda *refs: gather_kernel(chain, *refs), out_shape=jax.S...  34.4 us
    pallas_call x1, Pallas kernels, local(): pl.pallas_call(compute_kernel, out_shape=(jax.ShapeDtypeStruct((rows, WID...  23 us
    unnamed x19, local copies, waits for them, and re-layouts  10.9 us

profile of v1, /device:TPU:0, one launch (start us, length us, event | category | flops | bytes accessed | tf_op | source)
XLA Modules:
  0.0 161.1 jit_solution(9875698967716416926)
XLA Ops:
  0.6 0.0 copy-start
  0.7 0.0 copy-start.4
  0.7 0.0 copy-start.3
  1.4 0.8 slice.60
  2.2 0.7 broadcast_in_dim.6
  2.9 0.7 broadcast_in_dim.7
  3.7 0.1 maximum_bitcast_fusion.1
  3.8 1.5 copy.39.scol
  5.3 0.9 slice.61
  6.2 0.0 copy-start.1
  6.2 1.2 pad_maximum_fusion.2
  7.4 0.0 copy-start.2
  7.4 0.0 copy-done.3
  7.4 0.9 copy.37.x
  8.3 0.0 copy-done.4
  8.3 0.9 copy.38.cot
  9.2 0.0 copy-done
  9.2 0.5 reshape.71
  9.7 0.0 copy-done.1
  9.7 0.5 reshape.72
  10.2 0.0 copy-done.2
  10.2 0.5 reshape.70
  10.7 0.4 pad_maximum_fusion.1
  11.2 0.3 copy.36
  11.4 1.5 pad_maximum_fusion.refs_0_
  12.9 34.4 %gather.1.w = bf16[4,25,144,256]{3,2,1,0:T(8,128)(2,1)} custom-call(bf16[25,144,256]{2,1,0:T(8,128)(2,1)} %pad_maximum_fusion.refs_0_), custom_call_target="tpu_custom_call" | custom-call | tf_op jit(solution)/shard_map/gather/pallas_call | solution.py:603
  47.3 23.0 %layer.1 = (bf16[256,576]{1,0:T(8,128)(2,1)}, f32[256,576]{1,0:T(8,128)}, bf16[25,576,256]{2,1,0:T(8,128)(2,1)}) custom-call(bf16[256,576]{1,0:T(8,128)(2,1)} %copy.37.x, bf16[256,576]{1,0:T(8,128)(2,1)} %copy.38.cot, s32[1,256]{1,0:T(1,128)} %srow.1, s32[256,1]{1,0:T(8,128)} %copy.39.scol, s32[1,1]{1,0:T(1,128)} %bitcast.63.live, ...), custom_call_target="tpu_custom_call" | custom-call | tf_op jit(solution)/shard_map/layer/pallas_call | solution.py:614
  70.3 1.8 %copy.45 = bf16[256,576]{0,1:T(8,128)(2,1)} copy(bf16[256,576]{1,0:T(8,128)(2,1)} %get-tuple-element.28) | data formatting | bytes 589824
  72.2 2.1 %copy.46 = f32[256,576]{0,1:T(8,128)} copy(f32[256,576]{1,0:T(8,128)} %get-tuple-element.29) | data formatting | bytes 1179648
  74.3 75.7 %reduce.5 = f32[25,144,256]{2,1,0:T(8,128)} custom-call(bf16[25,576,256]{2,1,0:T(8,128)(2,1)} %get-tuple-element.16.refs_0_), custom_call_target="tpu_custom_call" | custom-call | tf_op jit(solution)/shard_map/reduce/pallas_call | solution.py:639
  150.0 0.9 slice_bitcast_fusion.2
  150.9 0.8 slice_reduce_fusion
  151.7 1.0 slice_bitcast_fusion.1
  152.7 0.8 maximum_bitcast_fusion
  153.5 1.1 slice_bitcast_fusion
  154.6 0.0 slice-start
  154.6 0.1 copy.52
  154.7 1.7 %slice-done = f32[18,144,256]{2,1,0:T(8,128)S(1)} async-done(((f32[25,144,256]{2,1,0:T(8,128)}), f32[18,144,256]{2,1,0:T(8,128)S(1)}, s32[]{:S(2)}) %slice-start) | async-done | bytes 2654232 | tf_op jit(solution)/shard_map/slice | solution.py:577
  156.3 0.2 fusion
  156.5 1.0 copy.56
  157.6 1.0 copy.55
  158.6 0.8 fusion.1
  159.3 0.8 slice.62
  160.1 1.0 copy.54
  (5 shorter events, 0.1 us)
Async XLA Ops:
  0.6 8.6 %copy-start = (bf16[144,1536]{1,0:T(8,128)(2,1)S(1)}, bf16[144,1536]{1,0:T(8,128)(2,1)}, u32[]{:S(2)}) copy-start(bf16[144,1536]{1,0:T(8,128)(2,1)} %param.21) | copy-start | bytes 1327108
  0.7 7.7 %copy-start.4 = (bf16[256,576]{0,1:T(8,128)(2,1)S(1)}, bf16[256,576]{0,1:T(8,128)(2,1)}, u32[]{:S(2)}) copy-start(bf16[256,576]{0,1:T(8,128)(2,1)} %param.16) | copy-start | bytes 884740
  0.7 6.8 %copy-start.3 = (bf16[256,576]{0,1:T(8,128)(2,1)S(1)}, bf16[256,576]{0,1:T(8,128)(2,1)}, u32[]{:S(2)}) copy-start(bf16[256,576]{0,1:T(8,128)(2,1)} %param.13) | copy-start | bytes 884740
  6.2 3.5 %copy-start.1 = (bf16[144,1536]{1,0:T(8,128)(2,1)S(1)}, bf16[144,1536]{1,0:T(8,128)(2,1)}, u32[]{:S(2)}) copy-start(bf16[144,1536]{1,0:T(8,128)(2,1)} %param.22) | copy-start | bytes 1327108
  7.4 2.8 %copy-start.2 = (bf16[1536,144]{0,1:T(8,128)(2,1)S(1)}, bf16[1536,144]{0,1:T(8,128)(2,1)}, u32[]{:S(2)}) copy-start(bf16[1536,144]{0,1:T(8,128)(2,1)} %param.23) | copy-start | bytes 1327108
  154.6 1.8 %slice-start = ((f32[25,144,256]{2,1,0:T(8,128)}), f32[18,144,256]{2,1,0:T(8,128)S(1)}, s32[]{:S(2)}) async-start(f32[25,144,256]{2,1,0:T(8,128)} %reduce.5), calls=%async_computation | async-start | bytes 5308416 | tf_op jit(solution)/shard_map/slice | solution.py:577
